TPU v7x, 256 devices: a whole 4x4x8 slice. The times are simulated.
256 devices in a mesh: req: 32 (over x, y, core), exp: 8 (over z).
Axes of the slice: x: 4, y: 4, z: 8, core: 2. Of those that a mesh axis runs over, the one named last changes fastest.
Arguments:
- residual: bfloat16 [4096, 2048], P(('req', 'exp')), may hold values from -12 to 12
- queries: bfloat16 [4096, 2, 2048], P('req', None, 'exp'), may hold values from -9 to 9
- kv_cache: bfloat16 [608, 2, 128, 2048], P('req', None, None, 'exp'), may hold values from -4 to 4
- page_table: int32 [288, 11], P('req'), may hold values from 0 to 18, as said below
- seq_lengths: int32 [288], P('req'), may hold values from 8 to 1408, as said below
- head_route: int32 [4096, 2], P('req'), may hold values from 0 to 7, all different within a row
- head_gate: float32 [4096, 2], P('req'), may hold values from 0.2 to 1
- out_weight: bfloat16 [8, 2048, 2048], P(None, 'exp'), may hold values from -0.5 to 0.5
- norm_gain: float32 [2048], replicated, may hold values from 0.25 to 1.75
- expert_route: int32 [4096, 2], P(('req', 'exp')), may hold values from 0 to 7, all different within a row; in each aligned block of 16 rows (0 to 15, 16 to 31, ...) at most 8 rows name the same one
- expert_gate: float32 [4096, 2], P(('req', 'exp')), may hold values from 0.2 to 1
- gate_up: bfloat16 [8, 2, 2048, 5632], P('exp', None, None, 'req'), may hold values from -0.125 to 0.125
- down_weight: bfloat16 [8, 5632, 2048], P('exp', 'req'), may hold values from -0.078125 to 0.078125
Outputs:
- attended: bfloat16 [4096, 2048], P(('req', 'exp'))
- expert_mix: bfloat16 [4096, 2048], P(('req', 'exp'))
Inputs may be any that keep to these rules, and one draw needn't show every extreme that they name: `page_table`: pages are numbered within the slot's group. A group's slot 0 lists 11 different pages; each other slot repeats one page along its row; no two slots of a group share a page. `seq_lengths`: slot 0 of every group is a prefill request of length at least 120; the other slots are decode requests of length at most 128. `head_route`: each row names 2 different attention experts. `expert_route`: each row names 2 different experts; within the rows of one device no expert is named by more than 8 rows.
All inputs are finite; a program needn't handle non-finite values.
Results may differ from a plain program's by a relative error of at most 0.023.
Values may be sent and summed in bfloat16 or wider, within the bound.
A program may use at most 128 MiB of HBM per device.

v0:
```python
import jax
import jax.numpy as jnp
from jax import lax
from jax.sharding import PartitionSpec as P

HD = 128
TOPA = 2
SPAN = 120


def attend_local(queries_one, key_rows, value_rows, positions, head_count):
    amount = queries_one.shape[0]
    heads_q = queries_one.reshape(amount * TOPA, head_count, HD)
    heads_k = key_rows.reshape(-1, head_count, HD)
    heads_v = value_rows.reshape(-1, head_count, HD)
    scores = jnp.einsum(
        "qhd,khd->hqk", heads_q, heads_k, preferred_element_type=jnp.float32
    ) * HD ** (-0.5)
    key_pos = jnp.arange(heads_k.shape[0], dtype=jnp.int32)
    row_pos = jnp.repeat(positions, TOPA)
    allowed = key_pos[None, :] <= row_pos[:, None]
    scores = jnp.where(allowed[None], scores, -1e30)
    row_max = jnp.max(scores, axis=2, keepdims=True)
    raised = jnp.exp(scores - row_max)
    attention_weights = (raised / jnp.sum(raised, axis=2, keepdims=True)).astype(jnp.bfloat16)
    mixture = jnp.einsum(
        "hqk,khd->qhd", attention_weights, heads_v, preferred_element_type=jnp.float32
    )
    return mixture.astype(jnp.bfloat16).reshape(amount, TOPA, head_count * HD)


def local(
    residual,
    queries,
    kv_cache,
    page_table,
    seq_lengths,
    head_route,
    head_gate,
    out_weight,
    norm_gain,
    expert_route,
    expert_gate,
    gate_up,
    down_weight,
):
    feature_width = queries.shape[2]
    head_count = feature_width // HD
    page_rows = kv_cache[page_table[0]]
    key_rows = page_rows[:, 0].reshape(-1, feature_width)
    value_rows = page_rows[:, 1].reshape(-1, feature_width)
    prefill_pos = seq_lengths[0] - SPAN + jnp.arange(SPAN, dtype=jnp.int32)
    prefill_out = attend_local(queries[:SPAN], key_rows, value_rows, prefill_pos, head_count)
    decode_pages = kv_cache[page_table[1:, 0]]

    def decode_one(query_row, page_block, length):
        return attend_local(
            query_row[None], page_block[0], page_block[1], (length - 1)[None], head_count
        )[0]

    decode_out = jax.vmap(decode_one)(queries[SPAN:], decode_pages, seq_lengths[1:])
    mixture = jnp.concatenate([prefill_out, decode_out], axis=0)
    partial_value = jnp.zeros((mixture.shape[0], residual.shape[1]), jnp.float32)
    for expert_index in range(out_weight.shape[0]):
        picked = head_route == expert_index
        chosen = jnp.sum(jnp.where(picked[:, :, None], mixture, jnp.zeros_like(mixture)), axis=1)
        weight = jnp.sum(jnp.where(picked, head_gate, jnp.zeros_like(head_gate)), axis=1)
        partial_value = partial_value + weight[:, None] * jnp.dot(
            chosen, out_weight[expert_index], preferred_element_type=jnp.float32
        )
    row_count = residual.shape[0]
    summed = lax.psum(partial_value.astype(jnp.bfloat16), "exp").astype(jnp.float32)
    own_heads = lax.dynamic_slice_in_dim(summed, lax.axis_index("exp") * row_count, row_count, 0)
    attended = (residual.astype(jnp.float32) + own_heads).astype(jnp.bfloat16)
    values_f = attended.astype(jnp.float32)
    normed = (
        values_f
        * lax.rsqrt(jnp.mean(values_f * values_f, axis=1, keepdims=True) + 1e-06)
        * norm_gain
    ).astype(jnp.bfloat16)
    experts = lax.axis_size("exp")
    capacity = max(2, 2 * TOPA * row_count // experts)
    flat_route = expert_route.reshape(-1)
    onehot = (flat_route[:, None] == jnp.arange(experts, dtype=jnp.int32)[None, :]).astype(
        jnp.int32
    )
    earlier = jnp.cumsum(onehot, axis=0) - onehot
    rank_index = jnp.sum(earlier * onehot, axis=1)
    slot_index = flat_route * capacity + rank_index
    placing = (
        jnp.arange(experts * capacity, dtype=jnp.int32)[:, None] == slot_index[None, :]
    ).astype(jnp.bfloat16)
    repeated = jnp.repeat(normed, TOPA, axis=0)
    outgoing = jnp.dot(placing, repeated, preferred_element_type=jnp.float32).astype(jnp.bfloat16)
    w_gate = gate_up[0, 0]
    w_up = gate_up[0, 1]
    w_down = down_weight[0]
    arrived = lax.all_to_all(outgoing, "exp", split_axis=0, concat_axis=0, tiled=True)
    portion = lax.all_gather(arrived, "req", axis=0, tiled=True)
    gate_part = jnp.dot(portion, w_gate, preferred_element_type=jnp.float32)
    up_part = jnp.dot(portion, w_up, preferred_element_type=jnp.float32)
    active = (jax.nn.silu(gate_part) * up_part).astype(jnp.bfloat16)
    portion = active
    returned = lax.psum_scatter(
        jnp.dot(portion, w_down, preferred_element_type=jnp.float32).astype(jnp.bfloat16),
        "req",
        scatter_dimension=0,
        tiled=True,
    )
    homeward = lax.all_to_all(returned, "exp", split_axis=0, concat_axis=0, tiled=True)
    picked_rows = jnp.take(homeward, slot_index, axis=0).astype(jnp.float32)
    weighted = picked_rows * expert_gate.reshape(-1)[:, None]
    expert_mix = jnp.sum(weighted.reshape(row_count, TOPA, -1), axis=1).astype(jnp.bfloat16)
    return (attended, expert_mix)


def solution(mesh):
    return jax.shard_map(
        local,
        mesh=mesh,
        in_specs=(
            P(("req", "exp"), None),
            P("req", None, "exp"),
            P("req", None, None, "exp"),
            P("req", None),
            P("req"),
            P("req", None),
            P("req", None),
            P(None, "exp", None),
            P(),
            P(("req", "exp"), None),
            P(("req", "exp"), None),
            P("exp", None, None, "req"),
            P("exp", "req", None),
        ),
        out_specs=(P(("req", "exp"), None), P(("req", "exp"), None)),
        check_vma=False,
    )
```

profile of v0, /device:TPU:2, one launch (start us, length us, event | category | flops | bytes accessed | tf_op | source)
XLA Modules:
  0.0 351.9 jit_solution(16315062266536121598)
XLA Ops:
  8.9 1.3 select_reduce_fusion.1
  15.4 1.8 gather_fusion
  17.2 2.4 fusion.83
  19.6 2.6 reshape_reshape_squeeze.7
  25.2 3.9 %fusion.86 = (f32[2,240]{1,0:T(2,128)S(1)}, f32[2,240,1408]{2,1,0:T(8,128)}) fusion(pred[240,1408]{1,0:T(8,128)(4,1)} %iota_compare_fusion, bf16[1408,2,128]{2,1,0:T(2,128)(2,1)} %reshape_reshape_squeeze.7, bf16[240,2,128]{2,1,0:T(2,128)(2,1)S(1)} %reshape.164), kind=kOutput, calls=%fused_computation.145 | convolution fusion | flops 175719808 | bytes 3886976 | tf_op jit(solution)/shard_map/sub | solution.py:24
  29.0 2.4 fusion.18
  38.5 2.2 fusion.85
  41.9 3.8 %fusion.63 = (bf16[128,256]{1,0:T(8,128)(2,1)S(1)}, bf16[128,256]{1,0:T(8,128)(2,1)S(1)}, bf16[128,256]{1,0:T(8,128)(2,1)S(1)}, bf16[128,256]{1,0:T(8,128)(2,1)S...) fusion(pred[128,2]{1,0:T(8,128)(4,1)} %copy.77, ...), kind=kLoop, calls=%fused_computation.90 | loop fusion | flops 851968 | bytes 657408 | tf_op jit(solution)/shard_map/reduce_sum | solution.py:66
  45.7 1.5 convolution_multiply_fusion.9
  47.3 1.5 fusion.13
  48.9 1.5 fusion.12
  50.4 1.5 fusion.11
  52.0 1.5 fusion.10
  53.6 1.5 fusion.9
  55.2 1.6 fusion.8
  56.7 2.4 fusion.14
  59.7 76.3 %all-reduce.2.cloned.1.call-done = bf16[128,2048]{1,0:T(8,128)(2,1)} async-done(((bf16[128,2048]{1,0:T(8,128)(2,1)}), bf16[128,2048]{1,0:T(8,128)(2,1)}) %all-reduce.2.cloned.1.call-update) | async-done | bytes 524304 | tf_op jit(solution)/shard_map/psum | solution.py:72
  137.4 14.4 %all_to_all.24 = bf16[8,8,2048]{2,1,0:T(8,128)(2,1)} all-to-all(bf16[8,8,2048]{2,1,0:T(8,128)(2,1)S(1)} %fusion.15), channel_id=1, replica_groups=mesh['req'=32,'exp'=8] {'exp'}, dimensions={0} | all-to-all | bytes 524288 | tf_op jit(solution)/shard_map/all_to_all | solution.py:98
  152.1 53.8 %all-gather.2.cloned.1.call-done = bf16[2048,2048]{1,0:T(8,128)(2,1)} async-done(((bf16[64,2048]{1,0:T(8,128)(2,1)}), bf16[2048,2048]{1,0:T(8,128)(2,1)}) %all-gather.2.cloned.1.call-update) | async-done | bytes 8388624 | tf_op jit(solution)/shard_map/all_gather | solution.py:99
  205.9 7.5 %fusion.43 = f32[2048,176]{0,1:T(8,128)} fusion(bf16[2048,2048]{1,0:T(8,128)(2,1)} %all-gather.2.cloned.1.call-done, bf16[1,2,2048,176]{2,3,1,0:T(8,128)(2,1)} %param.24), kind=kOutput, calls=%fused_computation.61 | convolution fusion | flops 1476395008 | bytes 10551296 | tf_op jit(solution)/shard_map/dot_general | solution.py:100
  213.5 12.5 %convolution_convert_fusion = bf16[2048,2048]{1,0:T(8,128)(2,1)} fusion(bf16[2048,2048]{1,0:T(8,128)(2,1)} %all-gather.2.cloned.1.call-done, f32[2048,176]{0,1:T(8,128)} %fusion.43, bf16[1,176,2048]{2,1,0:T(8,128)(2,1)} %param.25, bf16[1,2,2048,176]{2,3,1,0:T(8,128)(2,1)} %param.24), kind=kOutput, calls=%fused_computation.5 | convolution fusion | flops 2959147008 | bytes 19660800 | tf_op jit(solution)/shard_map/dot_general | solution.py:105
  226.4 99.6 %reduce-scatter.2.cloned.1.call-done = bf16[64,2048]{1,0:T(8,128)(2,1)} async-done(((bf16[2048,2048]{1,0:T(8,128)(2,1)}), bf16[64,2048]{1,0:T(8,128)(2,1)}) %reduce-scatter.2.cloned.1.call-update) | async-done | bytes 262160 | tf_op jit(solution)/shard_map/reduce_scatter | solution.py:104
  326.0 7.0 %all-to-all-start.1 = ((bf16[8,8,2048]{2,1,0:T(8,128)(2,1)}), bf16[8,8,2048]{2,1,0:T(8,128)(2,1)S(1)}, u32[]{:S(2)}, u32[]{:S(2)}) async-start(bf16[8,8,2048]{2,1,0:T(8,128)(2,1)} %bitcast.101), calls=%async_computation.2 | async-start | bytes 524288 | tf_op jit(solution)/shard_map/all_to_all | solution.py:110
  333.2 10.3 %all-to-all-done.1 = bf16[8,8,2048]{2,1,0:T(8,128)(2,1)S(1)} async-done(((bf16[8,8,2048]{2,1,0:T(8,128)(2,1)}), bf16[8,8,2048]{2,1,0:T(8,128)(2,1)S(1)}, u32[]{:S(2)}, u32[]{:S(2)}) %all-to-all-start.1) | async-done | bytes 262176 | tf_op jit(solution)/shard_map/all_to_all | solution.py:110
  (90 shorter events, 22.8 us)
Async XLA Ops:
  7.2 8.2 %copy-start = (bf16[19,2,128,256]{3,2,1,0:T(8,128)(2,1)S(1)}, bf16[19,2,128,256]{3,2,1,0:T(8,128)(2,1)}, u32[]{:S(2)}) copy-start(bf16[19,2,128,256]{3,2,1,0:T(8,128)(2,1)} %param.15) | copy-start | bytes 7471108
  7.2 128.8 %all-reduce.2.cloned.1.call-start = ((), (), s32[]{:S(2)}) async-start(), calls=%async_computation.3 | async-start | bytes 1048576 | tf_op jit(solution)/shard_map/psum | solution.py:72
  17.2 5.0 %copy-start.14 = (s32[9]{0:T(128)S(1)}, s32[9]{0:T(128)}, u32[]{:S(2)}) copy-start(s32[9]{0:T(128)} %param.17) | copy-start | bytes 112
  17.2 6.8 %slice-start = ((bf16[128,2,256]{2,1,0:T(2,128)(2,1)}), bf16[120,2,256]{2,1,0:T(2,128)(2,1)S(1)}, s32[]{:S(2)}) async-start(bf16[128,2,256]{2,1,0:T(2,128)(2,1)} %param.14), calls=%async_computation.6 | async-start | bytes 245760 | tf_op jit(solution)/shard_map/slice | solution.py:53
  25.2 3.9 %copy-start.1 = (bf16[1408,2,128]{2,1,0:T(2,128)(2,1)S(1)}, bf16[1408,2,128]{2,1,0:T(2,128)(2,1)}, u32[]{:S(2)}) copy-start(bf16[1408,2,128]{2,1,0:T(2,128)(2,1)} %reshape_reshape_squeeze.6) | copy-start | bytes 2162692
  40.8 6.5 %copy-start.12 = (f32[128]{0:T(128)S(1)}, f32[128]{0:T(128)}, u32[]{:S(2)}) copy-start(f32[128]{0:T(128)} %get-tuple-element.15) | copy-start | bytes 1540
  45.7 3.1 copy-start.11
  47.3 3.1 copy-start.10
  48.9 3.1 copy-start.9
  50.4 3.1 copy-start.8
  52.0 3.1 copy-start.7
  53.6 3.2 copy-start.6
  55.1 4.1 %copy-start.4 = (s32[16,2]{0,1:T(2,128)S(1)}, s32[16,2]{0,1:T(2,128)}, u32[]{:S(2)}) copy-start(s32[16,2]{0,1:T(2,128)} %param.22) | copy-start | bytes 388
  55.1 80.8 %copy-start.3 = (bf16[16,2048]{1,0:T(8,128)(2,1)S(1)}, bf16[16,2048]{1,0:T(8,128)(2,1)}, u32[]{:S(2)}) copy-start(bf16[16,2048]{1,0:T(8,128)(2,1)} %param.13) | copy-start | bytes 196612
  55.1 81.8 %copy-start.5 = (f32[2048]{0:T(1024)S(1)}, f32[2048]{0:T(1024)}, u32[]{:S(2)}) copy-start(f32[2048]{0:T(1024)} %param.21) | copy-start | bytes 24580
  59.1 146.8 %all-gather.2.cloned.1.call-start = ((), (), s32[]{:S(2)}) async-start(), calls=%async_computation.4 | async-start | bytes 8650752 | tf_op jit(solution)/shard_map/all_gather | solution.py:99
  137.0 76.5 %copy-start.2 = (bf16[16,2048]{1,0:T(8,128)(2,1)}, bf16[16,2048]{1,0:T(8,128)(2,1)S(1)}, u32[]{:S(2)}) copy-start(bf16[16,2048]{1,0:T(8,128)(2,1)S(1)} %get-tuple-element.19) | copy-start | bytes 196612
  151.9 174.1 %reduce-scatter.2.cloned.1.call-start = ((), (), s32[]{:S(2)}) async-start(), calls=%async_computation.5 | async-start | bytes 8650752 | tf_op jit(solution)/shard_map/reduce_scatter | solution.py:104
  226.0 107.1 %copy-start.13 = (f32[16,2]{0,1:T(2,128)S(1)}, f32[16,2]{0,1:T(2,128)}, u32[]{:S(2)}) copy-start(f32[16,2]{0,1:T(2,128)} %param.23) | copy-start | bytes 388
  326.0 17.5 %all-to-all-start.1 = ((bf16[8,8,2048]{2,1,0:T(8,128)(2,1)}), bf16[8,8,2048]{2,1,0:T(8,128)(2,1)S(1)}, u32[]{:S(2)}, u32[]{:S(2)}) async-start(bf16[8,8,2048]{2,1,0:T(8,128)(2,1)} %bitcast.101), calls=%async_computation.2 | async-start | bytes 524288 | tf_op jit(solution)/shard_map/all_to_all | solution.py:110
Sparse Core Ops, SparseCore 0:
  59.2 76.6 all-reduce.1
  152.0 53.8 all-gather.1
  226.2 99.7 reduce-scatter.1
where the time goes:
time: 353 us; the launch traced here: 352 us
  waiting for transfers between devices  240 us (68%)
  matrix products  43 us (12%)
  local copies, waits for them, and re-layouts  20.2 us (6%)
  blocking collectives  14.4 us (4%)
  between operations  14.1 us (4%)
  other arithmetic  12.8 us (4%)
  starting transfers between devices  7.29 us (2%)
    reduce_scatter x1, waiting for transfers between devices, local(): lax.psum_scatter(jnp.dot(portion, w_down, preferred_element_type=jnp.floa...  99.6 us
    psum x1, waiting for transfers between devices, local(): lax.psum(partial_value.astype(jnp.bfloat16), 'exp').astype(jnp.float32)  76.3 us
    all_gather x1, waiting for transfers between devices, local(): portion = lax.all_gather(arrived, 'req', axis=0, tiled=True)  53.8 us
    all_to_all x1, blocking collectives, local(): lax.all_to_all(outgoing, 'exp', split_axis=0, concat_axis=0, tiled=True)  14.4 us
    dot_general x8, matrix products, local(): jnp.dot(chosen, out_weight[expert_index], preferred_element_type=jnp.floa...  13.1 us
    dot_general x1, matrix products, local(): jnp.dot(portion, w_down, preferred_element_type=jnp.float32)  12.5 us
    all_to_all x1, waiting for transfers between devices, local(): lax.all_to_all(returned, 'exp', split_axis=0, concat_axis=0, tiled=True)  10.3 us
    dot_general x1, matrix products, local(): gate_part = jnp.dot(portion, w_gate, preferred_element_type=jnp.float32)  7.55 us
  transfers between devices with their start and end apart: 4, of which 4 were waited for; matrix products, arithmetic and copies ran while one was open for 0% of the time, Pallas kernels for 0%

commit v1 on v0

--- a/solution.py
+++ b/solution.py
@@ -96,7 +96,9 @@
     w_up = gate_up[0, 1]
     w_down = down_weight[0]
     arrived = lax.all_to_all(outgoing, "exp", split_axis=0, concat_axis=0, tiled=True)
-    portion = lax.all_gather(arrived, "req", axis=0, tiled=True)
+    portion = jnp.concatenate(
+        lax.all_to_all(jnp.stack([arrived] * lax.axis_size("req")), "req", 0, 0), axis=0
+    )
     gate_part = jnp.dot(portion, w_gate, preferred_element_type=jnp.float32)
     up_part = jnp.dot(portion, w_up, preferred_element_type=jnp.float32)
     active = (jax.nn.silu(gate_part) * up_part).astype(jnp.bfloat16)

time: 353 us -> 398 us (1.13)
  blocking collectives: 14.4 us -> 115 us
  waiting for transfers between devices: 240 us -> 182 us
  local copies, waits for them, and re-layouts: 20.2 us -> 24.5 us
    all_to_all x0 -> x1, blocking collectives: none -> 100 us  [local(): lax.all_to_all(jnp.stack([arrived] * lax.axis_size('req')), 'req', 0, 0)]
    all_gather x1 -> x0, waiting for transfers between devices: 53.8 us -> none  [local(): portion = lax.all_gather(arrived, 'req', axis=0, tiled=True)]
    reduce_scatter x1, waiting for transfers between devices: 99.6 us -> 95 us  [local(): lax.psum_scatter(jnp.dot(portion, w_down, preferred_element_type=jnp.floa...]
  transfers between devices with their start and end apart: 4 -> 3, of which waited for: 4 -> 3; matrix products, arithmetic and copies ran while one was open for 0% -> 0% of each run, Pallas kernels for 0% -> 0%
where the time goes in v1:
time: 398 us; the launch traced here: 396 us
  waiting for transfers between devices  182 us (46%)
  blocking collectives  115 us (29%)
  matrix products  41.2 us (10%)
  local copies, waits for them, and re-layouts  24.5 us (6%)
  between operations  14.5 us (4%)
  other arithmetic  12.8 us (3%)
  starting transfers between devices  7.11 us (2%)
    all_to_all x1, blocking collectives, local(): lax.all_to_all(jnp.stack([arrived] * lax.axis_size('req')), 'req', 0, 0)  100 us
    reduce_scatter x1, waiting for transfers between devices, local(): lax.psum_scatter(jnp.dot(portion, w_down, preferred_element_type=jnp.floa...  95 us
    psum x1, waiting for transfers between devices, local(): lax.psum(partial_value.astype(jnp.bfloat16), 'exp').astype(jnp.float32)  76.3 us
    all_to_all x1, blocking collectives, local(): lax.all_to_all(outgoing, 'exp', split_axis=0, concat_axis=0, tiled=True)  14.3 us
    dot_general x1, matrix products, local(): jnp.dot(portion, w_down, preferred_element_type=jnp.float32)  14.2 us
    dot_general x8, matrix products, local(): jnp.dot(chosen, out_weight[expert_index], preferred_element_type=jnp.floa...  13.1 us
    all_to_all x1, waiting for transfers between devices, local(): lax.all_to_all(returned, 'exp', split_axis=0, concat_axis=0, tiled=True)  10.3 us
  transfers between devices with their start and end apart: 3, of which 3 were waited for; matrix products, arithmetic and copies ran while one was open for 0% of the time, Pallas kernels for 0%

profile of v1, /device:TPU:2, one launch (start us, length us, event | category | flops | bytes accessed | tf_op | source)
XLA Modules:
  0.0 396.5 jit_solution(4595134699454261090)
XLA Ops:
  15.4 1.8 gather_fusion
  17.2 2.4 fusion.83
  19.6 2.6 reshape_reshape_squeeze.7
  25.2 3.9 fusion.86
  29.0 2.4 fusion.18
  38.5 2.2 fusion.85
  41.9 3.8 fusion.63
  45.7 1.5 convolution_multiply_fusion.9
  47.3 1.5 fusion.13
  48.9 1.5 fusion.12
  50.4 1.5 fusion.11
  52.0 1.5 fusion.10
  53.6 1.5 fusion.9
  55.2 1.6 fusion.8
  56.7 2.4 fusion.14
  59.7 76.3 %all-reduce.2.cloned.1.call-done = bf16[128,2048]{1,0:T(8,128)(2,1)} async-done(((bf16[128,2048]{1,0:T(8,128)(2,1)}), bf16[128,2048]{1,0:T(8,128)(2,1)}) %all-reduce.2.cloned.1.call-update) | async-done | bytes 524304 | tf_op jit(solution)/shard_map/psum | solution.py:72
  137.4 14.3 %all_to_all.26 = bf16[8,8,2048]{2,1,0:T(8,128)(2,1)S(1)} all-to-all(bf16[8,8,2048]{2,1,0:T(8,128)(2,1)S(1)} %fusion.15), channel_id=1, replica_groups=mesh['req'=32,'exp'=8] {'exp'}, dimensions={0} | all-to-all | bytes 524288 | tf_op jit(solution)/shard_map/all_to_all | solution.py:98
  152.8 100.4 %all_to_all.27 = bf16[32,64,2048]{2,1,0:T(8,128)(2,1)S(1)} all-to-all(bf16[32,64,2048]{2,1,0:T(8,128)(2,1)S(1)} %stack.5), channel_id=1, replica_groups=mesh['req'=32,'exp'=8] {'req'}, dimensions={0} | all-to-all | bytes 16777216 | tf_op jit(solution)/shard_map/all_to_all | solution.py:100
  253.2 3.2 copy-done.1
  256.5 4.0 %fusion.43 = f32[2048,176]{0,1:T(8,128)} fusion(bf16[2048,2048]{1,0:T(8,128)(2,1)S(1)} %bitcast.98, bf16[1,2,2048,176]{2,3,1,0:T(8,128)(2,1)S(1)} %copy-done.15), kind=kOutput, calls=%fused_computation.61 | convolution fusion | flops 1476395008 | bytes 10551296 | tf_op jit(solution)/shard_map/dot_general | solution.py:102
  260.5 14.2 %convolution_convert_fusion = bf16[2048,2048]{1,0:T(8,128)(2,1)} fusion(bf16[2048,2048]{1,0:T(8,128)(2,1)} %bitcast.99, f32[2048,176]{0,1:T(8,128)} %fusion.43, bf16[1,176,2048]{2,1,0:T(8,128)(2,1)S(1)} %copy-done.16, bf16[1,2,2048,176]{2,3,1,0:T(8,128)(2,1)} %param.24), kind=kOutput, calls=%fused_computation.5 | convolution fusion | flops 2959147008 | bytes 19660800 | tf_op jit(solution)/shard_map/dot_general | solution.py:107
  275.1 95.0 %reduce-scatter.2.cloned.1.call-done = bf16[64,2048]{1,0:T(8,128)(2,1)} async-done(((bf16[2048,2048]{1,0:T(8,128)(2,1)}), bf16[64,2048]{1,0:T(8,128)(2,1)}) %reduce-scatter.2.cloned.1.call-update) | async-done | bytes 262160 | tf_op jit(solution)/shard_map/reduce_scatter | solution.py:106
  370.2 7.0 %all-to-all-start.2 = ((bf16[8,8,2048]{2,1,0:T(8,128)(2,1)}), bf16[8,8,2048]{2,1,0:T(8,128)(2,1)S(1)}, u32[]{:S(2)}, u32[]{:S(2)}) async-start(bf16[8,8,2048]{2,1,0:T(8,128)(2,1)} %bitcast.104), calls=%async_computation.3 | async-start | bytes 524288 | tf_op jit(solution)/shard_map/all_to_all | solution.py:112
  377.4 10.3 %all-to-all-done.2 = bf16[8,8,2048]{2,1,0:T(8,128)(2,1)S(1)} async-done(((bf16[8,8,2048]{2,1,0:T(8,128)(2,1)}), bf16[8,8,2048]{2,1,0:T(8,128)(2,1)S(1)}, u32[]{:S(2)}, u32[]{:S(2)}) %all-to-all-start.2) | async-done | bytes 262176 | tf_op jit(solution)/shard_map/all_to_all | solution.py:112
  (95 shorter events, 24.9 us)
Async XLA Ops:
  7.2 8.2 %copy-start = (bf16[19,2,128,256]{3,2,1,0:T(8,128)(2,1)S(1)}, bf16[19,2,128,256]{3,2,1,0:T(8,128)(2,1)}, u32[]{:S(2)}) copy-start(bf16[19,2,128,256]{3,2,1,0:T(8,128)(2,1)} %param.15) | copy-start | bytes 7471108
  7.2 128.8 %all-reduce.2.cloned.1.call-start = ((), (), s32[]{:S(2)}) async-start(), calls=%async_computation.4 | async-start | bytes 1048576 | tf_op jit(solution)/shard_map/psum | solution.py:72
  17.2 5.0 %copy-start.17 = (s32[9]{0:T(128)S(1)}, s32[9]{0:T(128)}, u32[]{:S(2)}) copy-start(s32[9]{0:T(128)} %param.17) | copy-start | bytes 112
  17.2 6.8 %slice-start = ((bf16[128,2,256]{2,1,0:T(2,128)(2,1)}), bf16[120,2,256]{2,1,0:T(2,128)(2,1)S(1)}, s32[]{:S(2)}) async-start(bf16[128,2,256]{2,1,0:T(2,128)(2,1)} %param.14), calls=%async_computation.6 | async-start | bytes 245760 | tf_op jit(solution)/shard_map/slice | solution.py:53
  25.2 3.9 copy-start.2
  40.8 6.5 %copy-start.13 = (f32[128]{0:T(128)S(1)}, f32[128]{0:T(128)}, u32[]{:S(2)}) copy-start(f32[128]{0:T(128)} %get-tuple-element.15) | copy-start | bytes 1540
  45.7 3.1 copy-start.12
  47.3 3.1 copy-start.11
  48.9 3.1 copy-start.10
  50.4 3.1 copy-start.9
  52.0 3.1 copy-start.8
  53.6 3.2 copy-start.7
  55.1 4.1 %copy-start.5 = (s32[16,2]{0,1:T(2,128)S(1)}, s32[16,2]{0,1:T(2,128)}, u32[]{:S(2)}) copy-start(s32[16,2]{0,1:T(2,128)} %param.22) | copy-start | bytes 388
  55.1 80.8 %copy-start.4 = (bf16[16,2048]{1,0:T(8,128)(2,1)S(1)}, bf16[16,2048]{1,0:T(8,128)(2,1)}, u32[]{:S(2)}) copy-start(bf16[16,2048]{1,0:T(8,128)(2,1)} %param.13) | copy-start | bytes 196612
  55.1 81.8 %copy-start.6 = (f32[2048]{0:T(1024)S(1)}, f32[2048]{0:T(1024)}, u32[]{:S(2)}) copy-start(f32[2048]{0:T(1024)} %param.21) | copy-start | bytes 24580
  59.1 311.1 %reduce-scatter.2.cloned.1.call-start = ((), (), s32[]{:S(2)}) async-start(), calls=%async_computation.5 | async-start | bytes 8650752 | tf_op jit(solution)/shard_map/reduce_scatter | solution.py:106
  137.0 15.8 %copy-start.3 = (bf16[16,2048]{1,0:T(8,128)(2,1)}, bf16[16,2048]{1,0:T(8,128)(2,1)S(1)}, u32[]{:S(2)}) copy-start(bf16[16,2048]{1,0:T(8,128)(2,1)S(1)} %get-tuple-element.19) | copy-start | bytes 196612
  152.8 103.6 %copy-start.15 = (bf16[1,2,2048,176]{2,3,1,0:T(8,128)(2,1)S(1)}, bf16[1,2,2048,176]{2,3,1,0:T(8,128)(2,1)}, u32[]{:S(2)}) copy-start(bf16[1,2,2048,176]{2,3,1,0:T(8,128)(2,1)} %param.24) | copy-start | bytes 4325380
  253.2 3.2 copy-start.1
  256.4 4.1 %copy-start.16 = (bf16[1,176,2048]{2,1,0:T(8,128)(2,1)S(1)}, bf16[1,176,2048]{2,1,0:T(8,128)(2,1)}, u32[]{:S(2)}) copy-start(bf16[1,176,2048]{2,1,0:T(8,128)(2,1)} %param.25) | copy-start | bytes 2162692
  274.8 102.6 %copy-start.14 = (f32[16,2]{0,1:T(2,128)S(1)}, f32[16,2]{0,1:T(2,128)}, u32[]{:S(2)}) copy-start(f32[16,2]{0,1:T(2,128)} %param.23) | copy-start | bytes 388
  370.2 17.5 %all-to-all-start.2 = ((bf16[8,8,2048]{2,1,0:T(8,128)(2,1)}), bf16[8,8,2048]{2,1,0:T(8,128)(2,1)S(1)}, u32[]{:S(2)}, u32[]{:S(2)}) async-start(bf16[8,8,2048]{2,1,0:T(8,128)(2,1)} %bitcast.104), calls=%async_computation.3 | async-start | bytes 524288 | tf_op jit(solution)/shard_map/all_to_all | solution.py:112
Sparse Core Ops, SparseCore 0:
  59.2 76.6 all-reduce.1
  274.9 95.2 reduce-scatter.1
